TPU v7x, 256 devices: a whole 4x4x8 slice. The times are simulated.
256 devices in a mesh: band: 16 (over z, y_lo), pw: 16 (over x, y_hi, core).
Axes of the slice: x: 4, y: 4 (y_hi: 2, y_lo: 2; y = y_hi * 2 + y_lo), z: 8, core: 2. Of those that a mesh axis runs over, the one named last changes fastest.
Arguments:
- orbitals: bfloat16 [32, 192, 192, 256], P('band', 'pw'), may hold values from -5 to 5
- owner_group: int32 [1], replicated, may hold values from 0 to 15
Outputs:
- exchange_rows: float32 [32, 192, 192, 256], P('band', 'pw')
- owner_update: float32 [1, 192, 192, 256], P(None, 'pw', 'band')
All inputs are finite; a program needn't handle non-finite values.
Results may differ from a plain program's by a relative error of at most 0.0003.
Values may be sent and summed in bfloat16 or wider, within the bound.
A program may use at most 128 MiB of HBM per device.

v0:
```python
import math

import jax
import jax.numpy as jnp
from jax import lax
from jax.sharding import PartitionSpec as P

NX = 192
NY = 192
NZ = 256
SENT = 1


exact_share = 0.25
spacing = 0.2
highest = lax.Precision.HIGHEST


def broadcast(block, axis, owner):
    block = jnp.where(lax.axis_index(axis) == owner, block, jnp.zeros_like(block))
    return lax.psum(block, axis)


def dft_tables(length, number):
    samples = jnp.arange(length, dtype=jnp.int32)
    frequency = jnp.arange(number, dtype=jnp.int32)
    phase_index = samples[:, None] * frequency[None, :] % length
    phase_angle = phase_index.astype(jnp.float32) * (2 * math.pi / length)
    return (jnp.cos(phase_angle), jnp.sin(phase_angle))


def alternating(length):
    samples = jnp.arange(length, dtype=jnp.int32)
    return (1 - 2 * (samples % 2)).astype(jnp.float32)


def coulomb_table(ky_first, rows_y):
    freq_x = jnp.arange(NX, dtype=jnp.int32)
    freq_x = jnp.where(freq_x > NX // 2, freq_x - NX, freq_x)
    freq_y = ky_first + jnp.arange(rows_y, dtype=jnp.int32)
    freq_y = jnp.where(freq_y > NY // 2, freq_y - NY, freq_y)
    freq_z = jnp.arange(NZ // 2 + 1, dtype=jnp.int32)
    wave_x = freq_x.astype(jnp.float32) * (2 * math.pi / (NX * spacing))
    wave_y = freq_y.astype(jnp.float32) * (2 * math.pi / (NY * spacing))
    wave_z = freq_z.astype(jnp.float32) * (2 * math.pi / (NZ * spacing))
    square = (
        (wave_x * wave_x)[:, None, None]
        + (wave_y * wave_y)[None, :, None]
        + (wave_z * wave_z)[None, None, :]
    )
    safe = jnp.where(square > 0, square, 1.0)
    return jnp.where(square > 0, 4 * math.pi / safe, 0.0)


def complex_pass(spectrum, cosine_table, sine_table, pattern, direction):
    half_width = spectrum.shape[-1] // 2
    with_cosine = jnp.einsum(pattern, cosine_table, spectrum, precision=highest)
    with_sine = jnp.einsum(pattern, sine_table, spectrum, precision=highest)
    real_part = with_cosine[..., :half_width] + direction * with_sine[..., half_width:]
    imag_part = with_cosine[..., half_width:] - direction * with_sine[..., :half_width]
    return jnp.concatenate([real_part, imag_part], -1)


def split_pass(real_in, imag_in, cosine_table, sine_table, pattern, direction):
    real_part = jnp.einsum(
        pattern, cosine_table, real_in, precision=highest
    ) + direction * jnp.einsum(pattern, sine_table, imag_in, precision=highest)
    imag_part = jnp.einsum(
        pattern, cosine_table, imag_in, precision=highest
    ) - direction * jnp.einsum(pattern, sine_table, real_in, precision=highest)
    return (real_part, imag_part)


def forward_planes(density):
    cosine_z, sine_z = dft_tables(NZ, NZ // 2)
    z_table = jnp.concatenate([cosine_z, -sine_z], 1)
    spectrum = jnp.einsum("pxyz,zc->pxyc", density, z_table, precision=highest)
    nyquist = jnp.einsum("pxyz,z->pxy", density, alternating(NZ), precision=highest)
    cosine_y, sine_y = dft_tables(NY, NY)
    spectrum = complex_pass(spectrum, cosine_y, sine_y, "uy,pxyc->pxuc", 1.0)
    nyq_real, nyq_imag = split_pass(
        nyquist, jnp.zeros_like(nyquist), cosine_y, sine_y, "uy,pxy->pxu", 1.0
    )
    return (spectrum, nyq_real, nyq_imag)


def column_work(columns, nyq_real, nyq_imag, ky_first, rows_y):
    cosine_x, sine_x = dft_tables(NX, NX)
    spectrum = complex_pass(columns, cosine_x, sine_x, "ux,pxyc->puyc", 1.0)
    nyq_real, nyq_imag = split_pass(nyq_real, nyq_imag, cosine_x, sine_x, "ux,pxy->puy", 1.0)
    kernel = coulomb_table(ky_first, rows_y)
    main_kernel = kernel[:, :, : NZ // 2]
    edge_kernel = kernel[:, :, NZ // 2][None]
    spectrum = spectrum * jnp.concatenate([main_kernel, main_kernel], -1)[None]
    spectrum = complex_pass(spectrum, cosine_x, sine_x, "ux,pxyc->puyc", -1.0)
    nyq_real, nyq_imag = split_pass(
        nyq_real * edge_kernel, nyq_imag * edge_kernel, cosine_x, sine_x, "ux,pxy->puy", -1.0
    )
    return (spectrum, nyq_real, nyq_imag)


def inverse_planes(spectrum, nyq_real, nyq_imag):
    cosine_y, sine_y = dft_tables(NY, NY)
    spectrum = complex_pass(spectrum, cosine_y, sine_y, "uy,pxyc->pxuc", -1.0)
    edge_real, edge_imag = split_pass(nyq_real, nyq_imag, cosine_y, sine_y, "uy,pxy->pxu", -1.0)
    frequency = jnp.arange(NZ // 2, dtype=jnp.int32)
    cosine_z, sine_z = dft_tables(NZ, NZ // 2)
    first = frequency == 0
    real_weight = jnp.where(first, 1.0, 2.0).astype(jnp.float32)
    imag_weight = jnp.where(first, 0.0, 2.0).astype(jnp.float32)
    z_table = jnp.concatenate(
        [real_weight[:, None] * cosine_z.T, -imag_weight[:, None] * sine_z.T], 0
    )
    z_table = z_table * (1.0 / (NX * NY * NZ))
    result = jnp.einsum("pxyc,cz->pxyz", spectrum, z_table, precision=highest)
    edge_table = alternating(NZ) * (1.0 / (NX * NY * NZ))
    return result + edge_real[..., None] * edge_table


def on_device(orbitals, owner_group):
    own_count = orbitals.shape[0]
    slab_rows = orbitals.shape[1]
    received = broadcast(orbitals[:SENT], "band", owner_group[0])
    sent_values = received.astype(jnp.float32)
    own_values = orbitals.astype(jnp.float32)
    density = (own_values[:, None] * sent_values[None, :]).reshape(
        own_count * SENT, slab_rows, NY, NZ
    )
    planes, plane_real, plane_imag = forward_planes(density)
    rows_y = NY // lax.axis_size("pw")
    ky_first = lax.axis_index("pw") * rows_y
    pieces = []
    real_pieces = []
    imag_pieces = []
    for pair_index in range(planes.shape[0]):
        upper = pair_index + 1
        columns, col_real, col_imag = (
            lax.all_to_all(planes[pair_index:upper], "pw", split_axis=2, concat_axis=1, tiled=True),
            lax.all_to_all(
                plane_real[pair_index:upper], "pw", split_axis=2, concat_axis=1, tiled=True
            ),
            lax.all_to_all(
                plane_imag[pair_index:upper], "pw", split_axis=2, concat_axis=1, tiled=True
            ),
        )
        worked = column_work(columns, col_real, col_imag, ky_first, rows_y)
        main_back, real_back, imag_back = (
            lax.all_to_all(worked[0], "pw", split_axis=1, concat_axis=2, tiled=True),
            lax.all_to_all(worked[1], "pw", split_axis=1, concat_axis=2, tiled=True),
            lax.all_to_all(worked[2], "pw", split_axis=1, concat_axis=2, tiled=True),
        )
        pieces.append(main_back)
        real_pieces.append(real_back)
        imag_pieces.append(imag_back)
    returned = jnp.concatenate(pieces, 0)
    back_real = jnp.concatenate(real_pieces, 0)
    back_imag = jnp.concatenate(imag_pieces, 0)
    potential = inverse_planes(returned, back_real, back_imag).reshape(
        own_count, SENT, slab_rows, NY, NZ
    )
    exchange_rows = -exact_share * jnp.sum(potential * sent_values[None], 1)
    partial_value = -exact_share * jnp.sum(potential * own_values[:, None], 0)
    owner_update = lax.psum_scatter(partial_value, "band", scatter_dimension=2, tiled=True)
    return (exchange_rows, owner_update)


def solution(mesh):
    placed = (P("band", "pw", None, None), P())
    return jax.shard_map(
        on_device,
        mesh=mesh,
        in_specs=placed,
        out_specs=(P("band", "pw", None, None), P(None, "pw", "band", None)),
        check_vma=False,
    )
```

profile of v0, /device:TPU:8, one launch (start us, length us, event | category | flops | bytes accessed | tf_op | source)
XLA Modules:
  0.0 572.9 jit_solution(14537349176392429986)
XLA Ops:
  13.9 140.6 %all-reduce.2.cloned.1.call-done = bf16[12,192,256]{2,1,0:T(8,128)(2,1)} async-done(((bf16[12,192,256]{2,1,0:T(8,128)(2,1)}), bf16[12,192,256]{2,1,0:T(8,128)(2,1)}) %all-reduce.2.cloned.1.call-update) | async-done | bytes 1179664 | tf_op jit(solution)/shard_map/psum | solution.py:21
  156.1 5.5 fusion.1
  161.6 7.6 %convolution_bitcast_fusion.2 = f32[2,12,192,256]{3,2,1,0:T(8,128)} fusion(f32[2,12,192,256]{3,2,1,0:T(8,128)S(1)} %fusion.1), kind=kOutput, calls=%fused_computation.37 | convolution fusion | flops 2718240768 | bytes 9437184 | tf_op jit(solution)/shard_map/uy,pxyc->pxuc/dot_general | solution.py:58
  169.2 7.7 %convolution_bitcast_fusion.3 = f32[2,12,192,256]{3,2,1,0:T(8,128)} fusion(f32[2,12,192,256]{3,2,1,0:T(8,128)S(1)} %fusion.1), kind=kOutput, calls=%fused_computation.38 | convolution fusion | flops 2718240768 | bytes 9437184 | tf_op jit(solution)/shard_map/uy,pxyc->pxuc/dot_general | solution.py:57
  176.9 4.3 fusion
  186.6 6.0 %all-to-all-start.4 = ((f32[16,1,144]{2,1,0:T(1,128)}), f32[16,1,144]{2,1,0:T(1,128)S(1)}, u32[]{:S(2)}, u32[]{:S(2)}) async-start(f32[16,1,144]{2,1,0:T(1,128)} %reshape.293), calls=%async_computation.4 | async-start | bytes 32768 | tf_op jit(solution)/shard_map/all_to_all | solution.py:139
  192.6 7.0 %slice_subtract_fusion = (f32[2,12,192,128]{3,2,1,0:T(8,128)}, f32[2,12,192,128]{3,2,1,0:T(8,128)}) fusion(f32[2,12,192,256]{3,2,1,0:T(8,128)} %convolution_bitcast_fusion.2, f32[2,12,192,256]{3,2,1,0:T(8,128)} %convolution_bitcast_fusion.3), kind=kLoop, calls=%fused_computation.23 | loop fusion | flops 1179648 | bytes 14155776 | tf_op jit(solution)/shard_map/sub | solution.py:60
  204.8 7.2 %all-to-all-start.5 = ((f32[16,1,144]{2,1,0:T(1,128)}), f32[16,1,144]{2,1,0:T(1,128)S(1)}, u32[]{:S(2)}, u32[]{:S(2)}) async-start(f32[16,1,144]{2,1,0:T(1,128)} %reshape.295), calls=%async_computation.5 | async-start | bytes 32768 | tf_op jit(solution)/shard_map/all_to_all | solution.py:142
  214.4 5.2 all-to-all-done.5
  225.5 5.2 all-to-all-done.7
  230.6 4.0 all-to-all-start.8
  237.0 5.1 all-to-all-done.8
  261.9 4.8 all-to-all-done.9
  272.9 4.8 all-to-all-done.11
  284.0 4.8 all-to-all-done.10
  292.3 4.1 pad_maximum_fusion
  300.8 7.2 %all-to-all-start.2 = ((f32[1,12,192,256]{3,0,1,2:T(1,128)}), f32[1,12,192,256]{3,0,1,2:T(1,128)}, u32[]{:S(2)}, u32[]{:S(2)}) async-start(f32[1,12,192,256]{3,0,1,2:T(1,128)} %copy.86), calls=%async_computation.2 | async-start | bytes 4718592 | tf_op jit(solution)/shard_map/all_to_all | solution.py:138
  308.0 5.5 copy.81
  313.5 26.6 %all-to-all-done.2 = f32[1,12,192,256]{3,0,1,2:T(1,128)} async-done(((f32[1,12,192,256]{3,0,1,2:T(1,128)}), f32[1,12,192,256]{3,0,1,2:T(1,128)}, u32[]{:S(2)}, u32[]{:S(2)}) %all-to-all-start.2) | async-done | bytes 2359328 | tf_op jit(solution)/shard_map/all_to_all | solution.py:138
  340.1 5.7 all-to-all-start
  354.1 4.2 reshape.253
  358.3 4.8 convolution_bitcast_fusion.6
  377.9 6.8 %all-to-all-start.3 = ((f32[1,192,12,256]{3,0,2,1:T(1,128)}), f32[1,192,12,256]{3,0,2,1:T(1,128)}, u32[]{:S(2)}, u32[]{:S(2)}) async-start(f32[1,192,12,256]{3,0,2,1:T(1,128)} %copy.89), calls=%async_computation.3 | async-start | bytes 4718592 | tf_op jit(solution)/shard_map/all_to_all | solution.py:148
  391.7 4.1 reshape.252
  395.8 4.8 convolution_bitcast_fusion.10
  416.8 5.7 all-to-all-start.1
  430.8 5.3 copy.90
  436.2 18.4 %all-to-all-done.1 = f32[1,192,12,256]{3,0,2,1:T(1,128)} async-done(((f32[1,192,12,256]{3,0,2,1:T(1,128)}), f32[1,192,12,256]{3,0,2,1:T(1,128)}, u32[]{:S(2)}, u32[]{:S(2)}) %all-to-all-start.1) | async-done | bytes 2359328 | tf_op jit(solution)/shard_map/all_to_all | solution.py:148
  460.4 5.8 %convolution_bitcast_fusion = f32[2,12,192,256]{3,2,1,0:T(8,128)S(1)} fusion(f32[2,12,192,256]{3,2,1,0:T(8,128)S(1)} %copy_dynamic-update-slice_fusion), kind=kOutput, calls=%fused_computation.35 | convolution fusion | flops 2718240768 | bytes 9437184 | tf_op jit(solution)/shard_map/uy,pxyc->pxuc/dot_general | solution.py:58
  466.2 5.6 convolution_bitcast_fusion.1
  473.5 6.4 %fusion.2 = (f32[12,192,256]{2,1,0:T(8,128)S(1)}, f32[2,12,192,256]{3,2,1,0:T(8,128)}) fusion(bf16[2,12,192,256]{3,2,1,0:T(8,128)(2,1)S(1)} %copy-done.1, f32[256]{0:T(256)S(1)} %broadcast_multiply_fusion, f32[2,12,192]{2,1,0:T(8,128)S(1)} %fusion.23, f32[12,192,256]{2,1,0:T(8,128)S(1)} %mul.580, f32[128,256]{1,0:T(8,128)S(1)} %get-tuple-element.28, ...), kind=kOutput, calls=%fused_computation.4 | convolution fusion | flops 3632857088 | bytes 16796672 | tf_op jit(solution)/shard_map/pxyc,cz->pxyz/dot_general | solution.py:115
  483.2 80.9 %reduce-scatter.2.cloned.1.call-done = f32[1,12,12,256]{3,1,0,2:T(8,128)} async-done(((f32[1,12,192,256]{3,1,0,2:T(8,128)}), f32[1,12,12,256]{3,1,0,2:T(8,128)}) %reduce-scatter.2.cloned.1.call-update) | async-done | bytes 147472 | tf_op jit(solution)/shard_map/reduce_scatter | solution.py:163
  (175 shorter events, 135.4 us)
Async XLA Ops:
  7.2 147.4 %all-reduce.2.cloned.1.call-start = ((), (), s32[]{:S(2)}) async-start(), calls=%async_computation.13 | async-start | bytes 2359296 | tf_op jit(solution)/shard_map/psum | solution.py:21
  12.5 1.4 copy-start.4
  169.2 7.7 %copy-start = (bf16[2,12,192,256]{3,2,1,0:T(8,128)(2,1)S(1)}, bf16[2,12,192,256]{3,2,1,0:T(8,128)(2,1)}, u32[]{:S(2)}) copy-start(bf16[2,12,192,256]{3,2,1,0:T(8,128)(2,1)} %param.2) | copy-start | bytes 7077892
  186.6 18.1 %all-to-all-start.4 = ((f32[16,1,144]{2,1,0:T(1,128)}), f32[16,1,144]{2,1,0:T(1,128)S(1)}, u32[]{:S(2)}, u32[]{:S(2)}) async-start(f32[16,1,144]{2,1,0:T(1,128)} %reshape.293), calls=%async_computation.4 | async-start | bytes 32768 | tf_op jit(solution)/shard_map/all_to_all | solution.py:139
  204.8 14.8 %all-to-all-start.5 = ((f32[16,1,144]{2,1,0:T(1,128)}), f32[16,1,144]{2,1,0:T(1,128)S(1)}, u32[]{:S(2)}, u32[]{:S(2)}) async-start(f32[16,1,144]{2,1,0:T(1,128)} %reshape.295), calls=%async_computation.5 | async-start | bytes 32768 | tf_op jit(solution)/shard_map/all_to_all | solution.py:142
  219.6 11.0 %all-to-all-start.7 = ((f32[16,1,144]{2,1,0:T(1,128)}), f32[16,1,144]{2,1,0:T(1,128)S(1)}, u32[]{:S(2)}, u32[]{:S(2)}) async-start(f32[16,1,144]{2,1,0:T(1,128)} %reshape.287), calls=%async_computation.7 | async-start | bytes 32768 | tf_op jit(solution)/shard_map/all_to_all | solution.py:139
  230.6 11.5 %all-to-all-start.8 = ((f32[16,1,144]{2,1,0:T(1,128)}), f32[16,1,144]{2,1,0:T(1,128)S(1)}, u32[]{:S(2)}, u32[]{:S(2)}) async-start(f32[16,1,144]{2,1,0:T(1,128)} %reshape.289), calls=%async_computation.8 | async-start | bytes 32768 | tf_op jit(solution)/shard_map/all_to_all | solution.py:142
  255.5 11.2 %all-to-all-start.9 = ((f32[16,1,144]{2,1,0:T(1,128)}), f32[16,1,144]{2,1,0:T(1,128)S(1)}, u32[]{:S(2)}, u32[]{:S(2)}) async-start(f32[16,1,144]{2,1,0:T(1,128)} %reshape.291), calls=%async_computation.9 | async-start | bytes 32768 | tf_op jit(solution)/shard_map/all_to_all | solution.py:149
  266.7 11.0 %all-to-all-start.11 = ((f32[16,1,144]{2,1,0:T(1,128)}), f32[16,1,144]{2,1,0:T(1,128)S(1)}, u32[]{:S(2)}, u32[]{:S(2)}) async-start(f32[16,1,144]{2,1,0:T(1,128)} %reshape.299), calls=%async_computation.11 | async-start | bytes 32768 | tf_op jit(solution)/shard_map/all_to_all | solution.py:150
  277.7 18.7 %copy-start.6 = (f32[16,1,144]{2,1,0:T(1,128)}, f32[16,1,144]{2,1,0:T(1,128)S(1)}, u32[]{:S(2)}) copy-start(f32[16,1,144]{2,1,0:T(1,128)S(1)} %all-to-all-done.11) | copy-start | bytes 27652
  277.7 11.0 %all-to-all-start.10 = ((f32[16,1,144]{2,1,0:T(1,128)}), f32[16,1,144]{2,1,0:T(1,128)S(1)}, u32[]{:S(2)}, u32[]{:S(2)}) async-start(f32[16,1,144]{2,1,0:T(1,128)} %reshape.301), calls=%async_computation.10 | async-start | bytes 32768 | tf_op jit(solution)/shard_map/all_to_all | solution.py:150
  288.8 7.6 %copy-start.8 = (f32[16,1,144]{2,1,0:T(1,128)}, f32[16,1,144]{2,1,0:T(1,128)S(1)}, u32[]{:S(2)}) copy-start(f32[16,1,144]{2,1,0:T(1,128)S(1)} %all-to-all-done.10) | copy-start | bytes 27652
  288.8 11.4 %all-to-all-start.6 = ((f32[16,1,144]{2,1,0:T(1,128)}), f32[16,1,144]{2,1,0:T(1,128)S(1)}, u32[]{:S(2)}, u32[]{:S(2)}) async-start(f32[16,1,144]{2,1,0:T(1,128)} %reshape.297), calls=%async_computation.6 | async-start | bytes 32768 | tf_op jit(solution)/shard_map/all_to_all | solution.py:149
  300.2 0.6 copy-start.10
  300.8 39.3 %all-to-all-start.2 = ((f32[1,12,192,256]{3,0,1,2:T(1,128)}), f32[1,12,192,256]{3,0,1,2:T(1,128)}, u32[]{:S(2)}, u32[]{:S(2)}) async-start(f32[1,12,192,256]{3,0,1,2:T(1,128)} %copy.86), calls=%async_computation.2 | async-start | bytes 4718592 | tf_op jit(solution)/shard_map/all_to_all | solution.py:138
  340.1 37.8 %all-to-all-start = ((f32[1,12,192,256]{3,0,1,2:T(1,128)}), f32[1,12,192,256]{3,0,1,2:T(1,128)}, u32[]{:S(2)}, u32[]{:S(2)}) async-start(f32[1,12,192,256]{3,0,1,2:T(1,128)} %copy.81), calls=%async_computation | async-start | bytes 4718592 | tf_op jit(solution)/shard_map/all_to_all | solution.py:138
  358.3 4.9 copy-start.2
  377.9 39.0 %all-to-all-start.3 = ((f32[1,192,12,256]{3,0,2,1:T(1,128)}), f32[1,192,12,256]{3,0,2,1:T(1,128)}, u32[]{:S(2)}, u32[]{:S(2)}) async-start(f32[1,192,12,256]{3,0,2,1:T(1,128)} %copy.89), calls=%async_computation.3 | async-start | bytes 4718592 | tf_op jit(solution)/shard_map/all_to_all | solution.py:148
  395.8 4.9 copy-start.3
  415.0 9.5 %copy-start.7 = (f32[16,1,144]{2,1,0:T(1,128)S(1)}, f32[16,1,144]{2,1,0:T(1,128)}, u32[]{:S(2)}) copy-start(f32[16,1,144]{2,1,0:T(1,128)} %copy-done.6) | copy-start | bytes 27652
  415.0 10.9 %copy-start.9 = (f32[16,1,144]{2,1,0:T(1,128)S(1)}, f32[16,1,144]{2,1,0:T(1,128)}, u32[]{:S(2)}) copy-start(f32[16,1,144]{2,1,0:T(1,128)} %copy-done.8) | copy-start | bytes 27652
  415.0 12.3 %copy-start.11 = (f32[16,1,144]{2,1,0:T(1,128)S(1)}, f32[16,1,144]{2,1,0:T(1,128)}, u32[]{:S(2)}) copy-start(f32[16,1,144]{2,1,0:T(1,128)} %copy-done.10) | copy-start | bytes 27652
  416.8 37.8 %all-to-all-start.1 = ((f32[1,192,12,256]{3,0,2,1:T(1,128)}), f32[1,192,12,256]{3,0,2,1:T(1,128)}, u32[]{:S(2)}, u32[]{:S(2)}) async-start(f32[1,192,12,256]{3,0,2,1:T(1,128)} %copy.84), calls=%async_computation.1 | async-start | bytes 4718592 | tf_op jit(solution)/shard_map/all_to_all | solution.py:148
  422.5 141.6 %reduce-scatter.2.cloned.1.call-start = ((), (), s32[]{:S(2)}) async-start(), calls=%async_computation.14 | async-start | bytes 3342336 | tf_op jit(solution)/shard_map/reduce_scatter | solution.py:163
  458.5 1.7 copy-start.5
  471.8 1.7 copy-start.1
Sparse Core Ops, SparseCore 0:
  11.2 143.3 all-reduce.1
  483.3 80.7 reduce-scatter.1
where the time goes:
time: 581 us; the launch traced here: 573 us
  waiting for transfers between devices  299 us (51%)
  matrix products  94.3 us (16%)
  local copies, waits for them, and re-layouts  72.4 us (12%)
  starting transfers between devices  60.2 us (10%)
  other arithmetic  31.6 us (5%)
  between operations  15.9 us (3%)
    psum x1, waiting for transfers between devices, broadcast(): return lax.psum(block, axis)  141 us
    reduce_scatter x1, waiting for transfers between devices, on_device(): lax.psum_scatter(partial_value, 'band', scatter_dimension=2, tiled=True)  80.9 us
    dot_general x6, matrix products, complex_pass(): with_sine = jnp.einsum(pattern, sine_table, spectrum, precision=highest)  29.3 us
    all_to_all x2, waiting for transfers between devices, on_device(): lax.all_to_all(planes[pair_index:upper], 'pw', split_axis=2, concat_axis=...  27 us
    dot_general x6, matrix products, complex_pass(): with_cosine = jnp.einsum(pattern, cosine_table, spectrum, precision=highest)  26.4 us
    all_to_all x2, waiting for transfers between devices, on_device(): lax.all_to_all(worked[0], 'pw', split_axis=1, concat_axis=2, tiled=True)  20.2 us
    unnamed x51, local copies, waits for them, and re-layouts  14.4 us
    all_to_all x4, local copies, waits for them, and re-layouts, on_device(): lax.all_to_all(planes[pair_index:upper], 'pw', split_axis=2, concat_axis=...  13.9 us
  transfers between devices with their start and end apart: 14, of which 12 were waited for; matrix products, arithmetic and copies ran while one was open for 21% of the time, Pallas kernels for 0%

commit v1 on v0

v1 whole, which is shorter than its diff:
```python
import math

import jax
import jax.numpy as jnp
from jax import lax
from jax.sharding import PartitionSpec as P

SENT = 1
CHUNKS = 4

exact_share = 0.25
spacing = 0.2
highest = lax.Precision.HIGHEST


def dft_tables(length, number):
    samples = jnp.arange(length, dtype=jnp.int32)
    frequency = jnp.arange(number, dtype=jnp.int32)
    phase_index = samples[:, None] * frequency[None, :] % length
    phase_angle = phase_index.astype(jnp.float32) * (2 * math.pi / length)
    return (jnp.cos(phase_angle), jnp.sin(phase_angle))


def signed(freq, length):
    return jnp.where(freq > length // 2, freq - length, freq)


def coulomb_table(nx, ny, nz, ky_first, rows_y, kz_first, cols_z):
    freq_x = signed(jnp.arange(nx, dtype=jnp.int32), nx)
    freq_y = signed(ky_first + jnp.arange(rows_y, dtype=jnp.int32), ny)
    freq_z = signed(kz_first + jnp.arange(cols_z, dtype=jnp.int32), nz)
    wave_x = freq_x.astype(jnp.float32) * (2 * math.pi / (nx * spacing))
    wave_y = freq_y.astype(jnp.float32) * (2 * math.pi / (ny * spacing))
    wave_z = freq_z.astype(jnp.float32) * (2 * math.pi / (nz * spacing))
    square = (
        (wave_x * wave_x)[:, None, None]
        + (wave_y * wave_y)[None, :, None]
        + (wave_z * wave_z)[None, None, :]
    )
    safe = jnp.where(square > 0, square, 1.0)
    return jnp.where(square > 0, 4 * math.pi / safe, 0.0)


def complex_pass(spectrum, cosine_table, sine_table, pattern, direction):
    half_width = spectrum.shape[-1] // 2
    with_cosine = jnp.einsum(pattern, cosine_table, spectrum, precision=highest)
    with_sine = jnp.einsum(pattern, sine_table, spectrum, precision=highest)
    real_part = with_cosine[..., :half_width] + direction * with_sine[..., half_width:]
    imag_part = with_cosine[..., half_width:] - direction * with_sine[..., :half_width]
    return jnp.concatenate([real_part, imag_part], -1)


def band_broadcast(block, owner, groups):
    rows = block.shape[0] * block.shape[1]
    pieces = block.reshape(groups, rows // groups, block.shape[2])
    received = lax.all_to_all(pieces, "band", 0, 0, tiled=True)
    mine = lax.dynamic_index_in_dim(received, owner, 0, keepdims=True)
    spread = jnp.broadcast_to(mine, pieces.shape)
    gathered = lax.all_to_all(spread, "band", 0, 0, tiled=True)
    return gathered.reshape(block.shape)


def band_reduce_scatter(partial, groups):
    slab_rows, ny, nz = partial.shape
    pieces = partial.reshape(slab_rows, groups, ny // groups, nz).transpose(1, 0, 2, 3)
    received = lax.all_to_all(pieces, "band", 0, 0, tiled=True)
    return jnp.sum(received, 0)


def on_device(orbitals, owner_group):
    slab_rows, ny, nz = orbitals.shape[1:]
    pw_size = lax.axis_size("pw")
    groups = lax.axis_size("band")
    nx = slab_rows * pw_size
    rows_y = ny // pw_size
    ky_first = lax.axis_index("pw") * rows_y
    width = nz // CHUNKS

    sent_values = band_broadcast(orbitals[0], owner_group[0], groups).astype(jnp.float32)
    own_values = orbitals.astype(jnp.float32)
    packed = jnp.concatenate(
        [own_values[0] * sent_values, own_values[1] * sent_values], -1
    )

    cosine_z, sine_z = dft_tables(nz, nz)
    forward_z = jnp.concatenate(
        [jnp.concatenate([cosine_z, -sine_z], 1), jnp.concatenate([sine_z, cosine_z], 1)], 0
    )
    scale = 1.0 / (nx * ny * nz)
    inverse_z = jnp.concatenate(
        [jnp.concatenate([cosine_z, sine_z], 1), jnp.concatenate([-sine_z, cosine_z], 1)], 0
    ) * scale
    cosine_y, sine_y = dft_tables(ny, ny)
    cosine_x, sine_x = dft_tables(nx, nx)

    result = None
    for chunk in range(CHUNKS):
        low = chunk * width
        columns = jnp.concatenate(
            [forward_z[:, low : low + width], forward_z[:, nz + low : nz + low + width]], 1
        )
        spectrum = jnp.einsum("xyz,zc->xyc", packed, columns, precision=highest)
        spectrum = complex_pass(spectrum, cosine_y, sine_y, "uy,xyc->xuc", 1.0)
        spectrum = lax.all_to_all(spectrum, "pw", 1, 0, tiled=True)
        spectrum = complex_pass(spectrum, cosine_x, sine_x, "ux,xyc->uyc", 1.0)
        kernel = coulomb_table(nx, ny, nz, ky_first, rows_y, low, width)
        spectrum = spectrum * jnp.concatenate([kernel, kernel], -1)
        spectrum = complex_pass(spectrum, cosine_x, sine_x, "ux,xyc->uyc", -1.0)
        spectrum = lax.all_to_all(spectrum, "pw", 0, 1, tiled=True)
        spectrum = complex_pass(spectrum, cosine_y, sine_y, "uy,xyc->xuc", -1.0)
        rows = jnp.concatenate(
            [inverse_z[low : low + width], inverse_z[nz + low : nz + low + width]], 0
        )
        part = jnp.einsum("xyc,cz->xyz", spectrum, rows, precision=highest)
        result = part if result is None else result + part

    potential = jnp.stack([result[..., :nz], result[..., nz:]])
    exchange_rows = -exact_share * (potential * sent_values[None])
    partial_value = -exact_share * jnp.sum(potential * own_values, 0)
    owner_update = band_reduce_scatter(partial_value, groups)[None]
    return (exchange_rows, owner_update)


def solution(mesh):
    placed = (P("band", "pw", None, None), P())
    return jax.shard_map(
        on_device,
        mesh=mesh,
        in_specs=placed,
        out_specs=(P("band", "pw", None, None), P(None, "pw", "band", None)),
        check_vma=False,
    )
```

time: 581 us -> 469 us (0.81)
  waiting for transfers between devices: 299 us -> 112 us
  blocking collectives: 0 us -> 77.2 us
  matrix products: 94.3 us -> 115 us
  between operations: 15.9 us -> 2.43 us
  local copies, waits for them, and re-layouts: 72.4 us -> 61.9 us
  other arithmetic: 31.6 us -> 39.2 us
    psum x1 -> x0, waiting for transfers between devices: 141 us -> none  [broadcast(): return lax.psum(block, axis)]
    reduce_scatter x1 -> x0, waiting for transfers between devices: 80.9 us -> none  [on_device(): lax.psum_scatter(partial_value, 'band', scatter_dimension=2, tiled=True)]
    all_to_all x0 -> x1, blocking collectives: none -> 77.2 us  [band_reduce_scatter(): received = lax.all_to_all(pieces, 'band', 0, 0, tiled=True)]
    all_to_all x12 -> x10, waiting for transfers between devices: 77.1 us -> 112 us  [the longest x4 35.8 us: on_device(): spectrum = lax.all_to_all(spectrum, 'pw', 0, 1, tiled=True)]
    dot_general x6 -> x16, matrix products: 26.4 us -> 41.8 us  [complex_pass(): with_cosine = jnp.einsum(pattern, cosine_table, spectrum, precision=highest)]
    add x3 -> x16, other arithmetic: 1.28 us -> 13.8 us  [complex_pass(): with_cosine[..., :half_width] + direction * with_sine[..., half_width:]]
    dot_general x6 -> x16, matrix products: 29.3 us -> 37.7 us  [complex_pass(): with_sine = jnp.einsum(pattern, sine_table, spectrum, precision=highest)]
    another operation x6 -> x1, local copies, waits for them, and re-layouts: 8.71 us -> 0.61 us  [on_device(): potential = jnp.stack([result[..., :nz], result[..., nz:]])]
  transfers between devices with their start and end apart: 14 -> 10, of which waited for: 12 -> 10; matrix products, arithmetic and copies ran while one was open for 21% -> 27% of each run, Pallas kernels for 0% -> 0%
where the time goes in v1:
time: 469 us; the launch traced here: 463 us
  matrix products  115 us (25%)
  waiting for transfers between devices  112 us (24%)
  blocking collectives  77.2 us (16%)
  local copies, waits for them, and re-layouts  61.9 us (13%)
  starting transfers between devices  55.6 us (12%)
  other arithmetic  39.2 us (8%)
    all_to_all x1, blocking collectives, band_reduce_scatter(): received = lax.all_to_all(pieces, 'band', 0, 0, tiled=True)  77.2 us
    dot_general x16, matrix products, complex_pass(): with_cosine = jnp.einsum(pattern, cosine_table, spectrum, precision=highest)  41.8 us
    dot_general x16, matrix products, complex_pass(): with_sine = jnp.einsum(pattern, sine_table, spectrum, precision=highest)  37.7 us
    all_to_all x4, waiting for transfers between devices, on_device(): spectrum = lax.all_to_all(spectrum, 'pw', 0, 1, tiled=True)  35.8 us
    all_to_all x1, waiting for transfers between devices, band_broadcast(): received = lax.all_to_all(pieces, 'band', 0, 0, tiled=True)  29.5 us
    all_to_all x4, waiting for transfers between devices, on_device(): spectrum = lax.all_to_all(spectrum, 'pw', 1, 0, tiled=True)  28.2 us
    all_to_all x4, starting transfers between devices, on_device(): spectrum = lax.all_to_all(spectrum, 'pw', 1, 0, tiled=True)  21.1 us
    all_to_all x4, starting transfers between devices, on_device(): spectrum = lax.all_to_all(spectrum, 'pw', 0, 1, tiled=True)  19.6 us
  transfers between devices with their start and end apart: 10, of which 10 were waited for; matrix products, arithmetic and copies ran while one was open for 27% of the time, Pallas kernels for 0%

profile of v1, /device:TPU:8, one launch (start us, length us, event | category | flops | bytes accessed | tf_op | source)
XLA Modules:
  0.0 463.3 jit_solution(2557203724748978828)
XLA Ops:
  3.0 9.9 %all-to-all-start = ((bf16[16,144,256]{2,1,0:T(8,128)(2,1)}), bf16[16,144,256]{2,1,0:T(8,128)(2,1)S(1)}, u32[]{:S(2)}, u32[]{:S(2)}) async-start(bf16[16,144,256]{2,1,0:T(8,128)(2,1)} %bitcast.2), calls=%async_computation | async-start | bytes 2359296 | tf_op jit(solution)/shard_map/all_to_all | solution.py:56
  13.6 29.5 %all-to-all-done = bf16[16,144,256]{2,1,0:T(8,128)(2,1)S(1)} async-done(((bf16[16,144,256]{2,1,0:T(8,128)(2,1)}), bf16[16,144,256]{2,1,0:T(8,128)(2,1)S(1)}, u32[]{:S(2)}, u32[]{:S(2)}) %all-to-all-start) | async-done | bytes 1179680 | tf_op jit(solution)/shard_map/all_to_all | solution.py:56
  44.2 5.0 %all-to-all-start.1 = ((bf16[16,144,256]{2,1,0:T(8,128)(2,1)}), bf16[16,144,256]{2,1,0:T(8,128)(2,1)S(1)}, u32[]{:S(2)}, u32[]{:S(2)}) async-start(bf16[16,144,256]{2,1,0:T(8,128)(2,1)} %broadcast_in_dim.18), calls=%async_computation.1 | async-start | bytes 2359296 | tf_op jit(solution)/shard_map/all_to_all | solution.py:59
  60.1 18.6 %all-to-all-done.1 = bf16[16,144,256]{2,1,0:T(8,128)(2,1)S(1)} async-done(((bf16[16,144,256]{2,1,0:T(8,128)(2,1)}), bf16[16,144,256]{2,1,0:T(8,128)(2,1)S(1)}, u32[]{:S(2)}, u32[]{:S(2)}) %all-to-all-start.1) | async-done | bytes 1179680 | tf_op jit(solution)/shard_map/all_to_all | solution.py:59
  82.0 4.1 fusion.5
  90.1 4.3 fusion.2
  100.4 4.1 fusion.3
  106.4 3.5 convolution_bitcast_fusion.7
  112.8 6.2 %all-to-all-start.2 = ((f32[12,192,128]{2,0,1:T(8,128)}), f32[12,192,128]{2,0,1:T(8,128)}, u32[]{:S(2)}, u32[]{:S(2)}) async-start(f32[12,192,128]{2,0,1:T(8,128)} %copy.20), calls=%async_computation.2 | async-start | bytes 3145728 | tf_op jit(solution)/shard_map/all_to_all | solution.py:104
  119.0 6.0 %fusion.4 = f32[12,192,128]{2,1,0:T(8,128)S(1)} fusion(f32[12,192,256]{2,1,0:T(8,128)} %copy-done, f32[12,192,256]{2,1,0:T(8,128)S(1)} %get-tuple-element.2, f32[512,64]{1,0:T(8,128)} %get-tuple-element.52, f32[512,64]{1,0:T(8,128)} %get-tuple-element.53), kind=kOutput, calls=%fused_computation.13 | convolution fusion | flops 1813184512 | bytes 6160384 | tf_op jit(solution)/shard_map/xyz,zc->xyc/dot_general | solution.py:102
  142.6 5.9 %all-to-all-start.8 = ((f32[12,192,128]{2,0,1:T(8,128)}), f32[12,192,128]{2,0,1:T(8,128)}, u32[]{:S(2)}, u32[]{:S(2)}) async-start(f32[12,192,128]{2,0,1:T(8,128)} %copy.38), calls=%async_computation.8 | async-start | bytes 3145728 | tf_op jit(solution)/shard_map/all_to_all | solution.py:104
  159.9 12.2 %all-to-all-done.8 = f32[12,192,128]{2,0,1:T(8,128)} async-done(((f32[12,192,128]{2,0,1:T(8,128)}), f32[12,192,128]{2,0,1:T(8,128)}, u32[]{:S(2)}, u32[]{:S(2)}) %all-to-all-start.8) | async-done | bytes 1179680 | tf_op jit(solution)/shard_map/all_to_all | solution.py:104
  172.1 4.6 all-to-all-start.6
  187.9 12.4 %all-to-all-done.6 = f32[12,192,128]{2,0,1:T(8,128)} async-done(((f32[12,192,128]{2,0,1:T(8,128)}), f32[12,192,128]{2,0,1:T(8,128)}, u32[]{:S(2)}, u32[]{:S(2)}) %all-to-all-start.6) | async-done | bytes 1179680 | tf_op jit(solution)/shard_map/all_to_all | solution.py:104
  200.3 4.4 all-to-all-start.4
  204.7 4.1 fusion.73
  215.9 4.1 fusion.97
  228.3 5.3 %all-to-all-start.3 = ((f32[192,12,128]{2,1,0:T(8,128)}), f32[192,12,128]{2,1,0:T(8,128)}, u32[]{:S(2)}, u32[]{:S(2)}) async-start(f32[192,12,128]{2,1,0:T(8,128)} %copy.23), calls=%async_computation.3 | async-start | bytes 3145728 | tf_op jit(solution)/shard_map/all_to_all | solution.py:109
  243.8 13.4 %all-to-all-done.3 = f32[192,12,128]{2,1,0:T(8,128)} async-done(((f32[192,12,128]{2,1,0:T(8,128)}), f32[192,12,128]{2,1,0:T(8,128)}, u32[]{:S(2)}, u32[]{:S(2)}) %all-to-all-start.3) | async-done | bytes 1179680 | tf_op jit(solution)/shard_map/all_to_all | solution.py:109
  257.2 4.6 all-to-all-start.9
  273.2 12.2 %all-to-all-done.9 = f32[192,12,128]{2,1,0:T(8,128)} async-done(((f32[192,12,128]{2,1,0:T(8,128)}), f32[192,12,128]{2,1,0:T(8,128)}, u32[]{:S(2)}, u32[]{:S(2)}) %all-to-all-start.9) | async-done | bytes 1179680 | tf_op jit(solution)/shard_map/all_to_all | solution.py:109
  285.4 4.6 all-to-all-start.7
  290.0 4.0 fusion.109
  313.6 5.1 %all-to-all-start.5 = ((f32[192,12,128]{2,1,0:T(8,128)}), f32[192,12,128]{2,1,0:T(8,128)}, u32[]{:S(2)}, u32[]{:S(2)}) async-start(f32[192,12,128]{2,1,0:T(8,128)} %copy.29), calls=%async_computation.5 | async-start | bytes 3145728 | tf_op jit(solution)/shard_map/all_to_all | solution.py:109
  334.7 7.5 %all-to-all-done.5 = f32[192,12,128]{2,1,0:T(8,128)} async-done(((f32[192,12,128]{2,1,0:T(8,128)}), f32[192,12,128]{2,1,0:T(8,128)}, u32[]{:S(2)}, u32[]{:S(2)}) %all-to-all-start.5) | async-done | bytes 1179680 | tf_op jit(solution)/shard_map/all_to_all | solution.py:109
  347.6 3.3 convolution_bitcast_fusion.8
  357.4 4.0 fusion.34
  361.5 4.2 fusion.38
  365.8 4.0 fusion.30
  369.8 4.8 %add_add_fusion = f32[12,192,512]{2,1,0:T(8,128)S(1)} fusion(f32[12,192,512]{2,1,0:T(8,128)S(1)} %fusion.38, f32[12,192,512]{2,1,0:T(8,128)S(1)} %fusion.30, f32[12,192,512]{2,1,0:T(8,128)S(1)} %fusion.34, f32[12,192,64]{2,1,0:T(8,128)S(1)} %get-tuple-element.9, f32[12,192,64]{2,1,0:T(8,128)S(1)} %get-tuple-element.8, f32[64,512]{1,0:T(8,128)S(1)} %copy-done.28, ...), kind=kOutput, calls=%fused_computation.4 | convolution fusion | flops 1815838720 | bytes 20316160 | tf_op jit(solution)/shard_map/xyc,cz->xyz/dot_general | solution.py:114
  377.0 3.4 multiply_reduce_fusion
  384.8 77.2 %all_to_all.159 = f32[16,12,12,256]{3,2,1,0:T(8,128)S(1)} all-to-all(f32[16,12,12,256]{3,2,1,0:T(8,128)S(1)} %copy.44), channel_id=1, replica_groups=mesh['band'=16,'pw'=16] {'band'}, dimensions={0} | all-to-all | bytes 4718592 | tf_op jit(solution)/shard_map/all_to_all | solution.py:66
  (171 shorter events, 164.7 us)
Async XLA Ops:
  3.0 40.1 %all-to-all-start = ((bf16[16,144,256]{2,1,0:T(8,128)(2,1)}), bf16[16,144,256]{2,1,0:T(8,128)(2,1)S(1)}, u32[]{:S(2)}, u32[]{:S(2)}) async-start(bf16[16,144,256]{2,1,0:T(8,128)(2,1)} %bitcast.2), calls=%async_computation | async-start | bytes 2359296 | tf_op jit(solution)/shard_map/all_to_all | solution.py:56
  44.2 5.0 %copy-start.1 = (bf16[2,12,192,256]{3,2,1,0:T(8,128)(2,1)S(1)}, bf16[2,12,192,256]{3,2,1,0:T(8,128)(2,1)}, u32[]{:S(2)}) copy-start(bf16[2,12,192,256]{3,2,1,0:T(8,128)(2,1)} %param.2) | copy-start | bytes 7077892
  44.2 34.5 %all-to-all-start.1 = ((bf16[16,144,256]{2,1,0:T(8,128)(2,1)}), bf16[16,144,256]{2,1,0:T(8,128)(2,1)S(1)}, u32[]{:S(2)}, u32[]{:S(2)}) async-start(bf16[16,144,256]{2,1,0:T(8,128)(2,1)} %broadcast_in_dim.18), calls=%async_computation.1 | async-start | bytes 2359296 | tf_op jit(solution)/shard_map/all_to_all | solution.py:59
  78.7 3.3 copy-start.9
  78.7 3.3 copy-start.25
  78.7 3.3 copy-start.26
  82.0 18.3 %copy-start = (f32[12,192,256]{2,1,0:T(8,128)}, f32[12,192,256]{2,1,0:T(8,128)S(1)}, u32[]{:S(2)}) copy-start(f32[12,192,256]{2,1,0:T(8,128)S(1)} %get-tuple-element.3) | copy-start | bytes 7077892
  97.3 3.0 copy-start.21
  97.3 3.0 copy-start.22
  112.8 29.8 %all-to-all-start.2 = ((f32[12,192,128]{2,0,1:T(8,128)}), f32[12,192,128]{2,0,1:T(8,128)}, u32[]{:S(2)}, u32[]{:S(2)}) async-start(f32[12,192,128]{2,0,1:T(8,128)} %copy.20), calls=%async_computation.2 | async-start | bytes 3145728 | tf_op jit(solution)/shard_map/all_to_all | solution.py:104
  119.0 6.0 %copy-start.4 = (f32[12,192,128]{2,1,0:T(8,128)S(1)}, f32[12,192,128]{2,1,0:T(8,128)}, u32[]{:S(2)}) copy-start(f32[12,192,128]{2,1,0:T(8,128)} %convolution_bitcast_fusion.2) | copy-start | bytes 3538948
  119.0 6.0 %copy-start.5 = (f32[12,192,128]{2,1,0:T(8,128)S(1)}, f32[12,192,128]{2,1,0:T(8,128)}, u32[]{:S(2)}) copy-start(f32[12,192,128]{2,1,0:T(8,128)} %convolution_bitcast_fusion.3) | copy-start | bytes 3538948
  142.6 29.5 %all-to-all-start.8 = ((f32[12,192,128]{2,0,1:T(8,128)}), f32[12,192,128]{2,0,1:T(8,128)}, u32[]{:S(2)}, u32[]{:S(2)}) async-start(f32[12,192,128]{2,0,1:T(8,128)} %copy.38), calls=%async_computation.8 | async-start | bytes 3145728 | tf_op jit(solution)/shard_map/all_to_all | solution.py:104
  172.1 28.2 %all-to-all-start.6 = ((f32[12,192,128]{2,0,1:T(8,128)}), f32[12,192,128]{2,0,1:T(8,128)}, u32[]{:S(2)}, u32[]{:S(2)}) async-start(f32[12,192,128]{2,0,1:T(8,128)} %copy.32), calls=%async_computation.6 | async-start | bytes 3145728 | tf_op jit(solution)/shard_map/all_to_all | solution.py:104
  200.3 28.0 %all-to-all-start.4 = ((f32[12,192,128]{2,0,1:T(8,128)}), f32[12,192,128]{2,0,1:T(8,128)}, u32[]{:S(2)}, u32[]{:S(2)}) async-start(f32[12,192,128]{2,0,1:T(8,128)} %copy.26), calls=%async_computation.4 | async-start | bytes 3145728 | tf_op jit(solution)/shard_map/all_to_all | solution.py:104
  204.7 4.1 copy-start.20
  215.9 4.1 copy-start.11
  225.9 7.7 %copy-start.19 = (f32[192,12,64]{2,0,1:T(8,128)S(1)}, f32[192,12,64]{2,0,1:T(8,128)}, u32[]{:S(2)}) copy-start(f32[192,12,64]{2,0,1:T(8,128)} %get-tuple-element.10) | copy-start | bytes 1769476
  228.3 28.9 %all-to-all-start.3 = ((f32[192,12,128]{2,1,0:T(8,128)}), f32[192,12,128]{2,1,0:T(8,128)}, u32[]{:S(2)}, u32[]{:S(2)}) async-start(f32[192,12,128]{2,1,0:T(8,128)} %copy.23), calls=%async_computation.3 | async-start | bytes 3145728 | tf_op jit(solution)/shard_map/all_to_all | solution.py:109
  257.2 28.1 %all-to-all-start.9 = ((f32[192,12,128]{2,1,0:T(8,128)}), f32[192,12,128]{2,1,0:T(8,128)}, u32[]{:S(2)}, u32[]{:S(2)}) async-start(f32[192,12,128]{2,1,0:T(8,128)} %copy.41), calls=%async_computation.9 | async-start | bytes 3145728 | tf_op jit(solution)/shard_map/all_to_all | solution.py:109
  285.4 28.2 %all-to-all-start.7 = ((f32[192,12,128]{2,1,0:T(8,128)}), f32[192,12,128]{2,1,0:T(8,128)}, u32[]{:S(2)}, u32[]{:S(2)}) async-start(f32[192,12,128]{2,1,0:T(8,128)} %copy.35), calls=%async_computation.7 | async-start | bytes 3145728 | tf_op jit(solution)/shard_map/all_to_all | solution.py:109
  301.1 4.6 copy-start.12
  313.6 28.7 %all-to-all-start.5 = ((f32[192,12,128]{2,1,0:T(8,128)}), f32[192,12,128]{2,1,0:T(8,128)}, u32[]{:S(2)}, u32[]{:S(2)}) async-start(f32[192,12,128]{2,1,0:T(8,128)} %copy.29), calls=%async_computation.5 | async-start | bytes 3145728 | tf_op jit(solution)/shard_map/all_to_all | solution.py:109
  326.8 3.0 copy-start.13
  347.6 3.3 copy-start.14
  357.4 4.0 copy-start.31
  357.4 4.0 copy-start.32
  361.4 4.3 copy-start.29
  361.5 4.3 copy-start.30
  365.7 4.1 copy-start.27
  365.7 4.1 copy-start.28
  374.6 2.4 copy-start.18
  (13 other events, 18.0 us)

commit v2 on v1

--- a/solution.py
+++ b/solution.py
@@ -14,7 +14,7 @@
 
 
 def dft_tables(length, number):
-    samples = jnp.arange(length, dtype=jnp.int32)
+    samples = lax.optimization_barrier(jnp.arange(length, dtype=jnp.int32))
     frequency = jnp.arange(number, dtype=jnp.int32)
     phase_index = samples[:, None] * frequency[None, :] % length
     phase_angle = phase_index.astype(jnp.float32) * (2 * math.pi / length)
@@ -62,9 +62,11 @@
 
 def band_reduce_scatter(partial, groups):
     slab_rows, ny, nz = partial.shape
-    pieces = partial.reshape(slab_rows, groups, ny // groups, nz).transpose(1, 0, 2, 3)
+    rows = ny // groups
+    pieces = partial.reshape(slab_rows, groups, rows, nz).transpose(1, 0, 2, 3)
+    pieces = pieces.reshape(groups, slab_rows * rows, nz)
     received = lax.all_to_all(pieces, "band", 0, 0, tiled=True)
-    return jnp.sum(received, 0)
+    return jnp.sum(received, 0).reshape(slab_rows, rows, nz)
 
 
 def on_device(orbitals, owner_group):

time: 469 us -> 455 us (0.970)
  blocking collectives: 77.2 us -> 60.5 us
  waiting for transfers between devices: 112 us -> 119 us
  other arithmetic: 39.2 us -> 33.8 us
    all_to_all x1, blocking collectives: 77.2 us -> 60.5 us  [band_reduce_scatter(): received = lax.all_to_all(pieces, 'band', 0, 0, tiled=True)]
    all_to_all x4, waiting for transfers between devices: 28.2 us -> 33.4 us  [on_device(): spectrum = lax.all_to_all(spectrum, 'pw', 1, 0, tiled=True)]
  transfers between devices with their start and end apart: 10 -> 10, of which waited for: 10 -> 10; matrix products, arithmetic and copies ran while one was open for 27% -> 26% of each run, Pallas kernels for 0% -> 0%
where the time goes in v2:
time: 455 us; the launch traced here: 451 us
  waiting for transfers between devices  119 us (26%)
  matrix products  116 us (25%)
  local copies, waits for them, and re-layouts  63.7 us (14%)
  blocking collectives  60.5 us (13%)
  starting transfers between devices  55.9 us (12%)
  other arithmetic  33.8 us (7%)
    all_to_all x1, blocking collectives, band_reduce_scatter(): received = lax.all_to_all(pieces, 'band', 0, 0, tiled=True)  60.5 us
    dot_general x16, matrix products, complex_pass(): with_cosine = jnp.einsum(pattern, cosine_table, spectrum, precision=highest)  42.5 us
    dot_general x16, matrix products, complex_pass(): with_sine = jnp.einsum(pattern, sine_table, spectrum, precision=highest)  37.1 us
    all_to_all x4, waiting for transfers between devices, on_device(): spectrum = lax.all_to_all(spectrum, 'pw', 0, 1, tiled=True)  36.1 us
    all_to_all x4, waiting for transfers between devices, on_device(): spectrum = lax.all_to_all(spectrum, 'pw', 1, 0, tiled=True)  33.4 us
    all_to_all x1, waiting for transfers between devices, band_broadcast(): received = lax.all_to_all(pieces, 'band', 0, 0, tiled=True)  29.5 us
    all_to_all x4, starting transfers between devices, on_device(): spectrum = lax.all_to_all(spectrum, 'pw', 1, 0, tiled=True)  21.8 us
    all_to_all x1, waiting for transfers between devices, band_broadcast(): gathered = lax.all_to_all(spread, 'band', 0, 0, tiled=True)  19.6 us
  transfers between devices with their start and end apart: 10, of which 10 were waited for; matrix products, arithmetic and copies ran while one was open for 26% of the time, Pallas kernels for 0%

profile of v2, /device:TPU:8, one launch (start us, length us, event | category | flops | bytes accessed | tf_op | source)
XLA Modules:
  0.0 450.6 jit_solution(14809800874012737659)
XLA Ops:
  3.0 9.9 %all-to-all-start = ((bf16[16,144,256]{2,1,0:T(8,128)(2,1)}), bf16[16,144,256]{2,1,0:T(8,128)(2,1)S(1)}, u32[]{:S(2)}, u32[]{:S(2)}) async-start(bf16[16,144,256]{2,1,0:T(8,128)(2,1)} %bitcast.2), calls=%async_computation | async-start | bytes 2359296 | tf_op jit(solution)/shard_map/all_to_all | solution.py:56
  13.6 29.5 %all-to-all-done = bf16[16,144,256]{2,1,0:T(8,128)(2,1)S(1)} async-done(((bf16[16,144,256]{2,1,0:T(8,128)(2,1)}), bf16[16,144,256]{2,1,0:T(8,128)(2,1)S(1)}, u32[]{:S(2)}, u32[]{:S(2)}) %all-to-all-start) | async-done | bytes 1179680 | tf_op jit(solution)/shard_map/all_to_all | solution.py:56
  44.2 5.0 %all-to-all-start.1 = ((bf16[16,144,256]{2,1,0:T(8,128)(2,1)}), bf16[16,144,256]{2,1,0:T(8,128)(2,1)S(1)}, u32[]{:S(2)}, u32[]{:S(2)}) async-start(bf16[16,144,256]{2,1,0:T(8,128)(2,1)} %broadcast_in_dim.16), calls=%async_computation.1 | async-start | bytes 2359296 | tf_op jit(solution)/shard_map/all_to_all | solution.py:59
  59.1 19.6 %all-to-all-done.1 = bf16[16,144,256]{2,1,0:T(8,128)(2,1)S(1)} async-done(((bf16[16,144,256]{2,1,0:T(8,128)(2,1)}), bf16[16,144,256]{2,1,0:T(8,128)(2,1)S(1)}, u32[]{:S(2)}, u32[]{:S(2)}) %all-to-all-start.1) | async-done | bytes 1179680 | tf_op jit(solution)/shard_map/all_to_all | solution.py:59
  82.1 4.1 fusion.5
  90.3 4.7 %fusion.2 = f32[12,192,128]{2,1,0:T(8,128)S(1)} fusion(f32[12,192,256]{2,1,0:T(8,128)S(1)} %get-tuple-element.3, f32[12,192,256]{2,1,0:T(8,128)S(1)} %get-tuple-element.2, f32[512,64]{1,0:T(8,128)S(1)} %copy-done.22, f32[512,64]{1,0:T(8,128)S(1)} %copy-done.21), kind=kOutput, calls=%fused_computation.11 | convolution fusion | flops 1813184512 | bytes 6160384 | tf_op jit(solution)/shard_map/xyz,zc->xyc/dot_general | solution.py:104
  101.1 4.1 fusion.3
  113.4 6.2 %all-to-all-start.2 = ((f32[12,192,128]{2,0,1:T(8,128)}), f32[12,192,128]{2,0,1:T(8,128)}, u32[]{:S(2)}, u32[]{:S(2)}) async-start(f32[12,192,128]{2,0,1:T(8,128)} %copy.21), calls=%async_computation.2 | async-start | bytes 3145728 | tf_op jit(solution)/shard_map/all_to_all | solution.py:106
  119.6 6.0 %fusion.4 = f32[12,192,128]{2,1,0:T(8,128)S(1)} fusion(f32[12,192,256]{2,1,0:T(8,128)} %copy-done, f32[12,192,256]{2,1,0:T(8,128)S(1)} %get-tuple-element.2, f32[512,64]{1,0:T(8,128)} %get-tuple-element.52, f32[512,64]{1,0:T(8,128)} %get-tuple-element.53), kind=kOutput, calls=%fused_computation.13 | convolution fusion | flops 1813184512 | bytes 6160384 | tf_op jit(solution)/shard_map/xyz,zc->xyc/dot_general | solution.py:104
  143.2 6.2 %all-to-all-start.8 = ((f32[12,192,128]{2,0,1:T(8,128)}), f32[12,192,128]{2,0,1:T(8,128)}, u32[]{:S(2)}, u32[]{:S(2)}) async-start(f32[12,192,128]{2,0,1:T(8,128)} %copy.39), calls=%async_computation.8 | async-start | bytes 3145728 | tf_op jit(solution)/shard_map/all_to_all | solution.py:106
  158.7 14.4 %all-to-all-done.8 = f32[12,192,128]{2,0,1:T(8,128)} async-done(((f32[12,192,128]{2,0,1:T(8,128)}), f32[12,192,128]{2,0,1:T(8,128)}, u32[]{:S(2)}, u32[]{:S(2)}) %all-to-all-start.8) | async-done | bytes 1179680 | tf_op jit(solution)/shard_map/all_to_all | solution.py:106
  173.1 4.8 %all-to-all-start.6 = ((f32[12,192,128]{2,0,1:T(8,128)}), f32[12,192,128]{2,0,1:T(8,128)}, u32[]{:S(2)}, u32[]{:S(2)}) async-start(f32[12,192,128]{2,0,1:T(8,128)} %copy.33), calls=%async_computation.6 | async-start | bytes 3145728 | tf_op jit(solution)/shard_map/all_to_all | solution.py:106
  177.9 4.1 fusion.115
  190.4 11.0 %all-to-all-done.6 = f32[12,192,128]{2,0,1:T(8,128)} async-done(((f32[12,192,128]{2,0,1:T(8,128)}), f32[12,192,128]{2,0,1:T(8,128)}, u32[]{:S(2)}, u32[]{:S(2)}) %all-to-all-start.6) | async-done | bytes 1179680 | tf_op jit(solution)/shard_map/all_to_all | solution.py:106
  201.4 4.6 %all-to-all-start.4 = ((f32[12,192,128]{2,0,1:T(8,128)}), f32[12,192,128]{2,0,1:T(8,128)}, u32[]{:S(2)}, u32[]{:S(2)}) async-start(f32[12,192,128]{2,0,1:T(8,128)} %copy.27), calls=%async_computation.4 | async-start | bytes 3145728 | tf_op jit(solution)/shard_map/all_to_all | solution.py:106
  222.6 7.0 %all-to-all-done.4 = f32[12,192,128]{2,0,1:T(8,128)} async-done(((f32[12,192,128]{2,0,1:T(8,128)}), f32[12,192,128]{2,0,1:T(8,128)}, u32[]{:S(2)}, u32[]{:S(2)}) %all-to-all-start.4) | async-done | bytes 1179680 | tf_op jit(solution)/shard_map/all_to_all | solution.py:106
  229.6 4.6 %all-to-all-start.3 = ((f32[192,12,128]{2,1,0:T(8,128)}), f32[192,12,128]{2,1,0:T(8,128)}, u32[]{:S(2)}, u32[]{:S(2)}) async-start(f32[192,12,128]{2,1,0:T(8,128)} %copy.24), calls=%async_computation.3 | async-start | bytes 3145728 | tf_op jit(solution)/shard_map/all_to_all | solution.py:111
  247.2 10.6 %all-to-all-done.3 = f32[192,12,128]{2,1,0:T(8,128)} async-done(((f32[192,12,128]{2,1,0:T(8,128)}), f32[192,12,128]{2,1,0:T(8,128)}, u32[]{:S(2)}, u32[]{:S(2)}) %all-to-all-start.3) | async-done | bytes 1179680 | tf_op jit(solution)/shard_map/all_to_all | solution.py:111
  257.8 4.7 %all-to-all-start.9 = ((f32[192,12,128]{2,1,0:T(8,128)}), f32[192,12,128]{2,1,0:T(8,128)}, u32[]{:S(2)}, u32[]{:S(2)}) async-start(f32[192,12,128]{2,1,0:T(8,128)} %copy.42), calls=%async_computation.9 | async-start | bytes 3145728 | tf_op jit(solution)/shard_map/all_to_all | solution.py:111
  270.0 16.0 %all-to-all-done.9 = f32[192,12,128]{2,1,0:T(8,128)} async-done(((f32[192,12,128]{2,1,0:T(8,128)}), f32[192,12,128]{2,1,0:T(8,128)}, u32[]{:S(2)}, u32[]{:S(2)}) %all-to-all-start.9) | async-done | bytes 1179680 | tf_op jit(solution)/shard_map/all_to_all | solution.py:111
  286.0 4.9 %all-to-all-start.7 = ((f32[192,12,128]{2,1,0:T(8,128)}), f32[192,12,128]{2,1,0:T(8,128)}, u32[]{:S(2)}, u32[]{:S(2)}) async-start(f32[192,12,128]{2,1,0:T(8,128)} %copy.36), calls=%async_computation.7 | async-start | bytes 3145728 | tf_op jit(solution)/shard_map/all_to_all | solution.py:111
  290.9 4.1 fusion.109
  308.7 3.3 convolution_bitcast_fusion.13
  314.4 5.1 %all-to-all-start.5 = ((f32[192,12,128]{2,1,0:T(8,128)}), f32[192,12,128]{2,1,0:T(8,128)}, u32[]{:S(2)}, u32[]{:S(2)}) async-start(f32[192,12,128]{2,1,0:T(8,128)} %copy.30), calls=%async_computation.5 | async-start | bytes 3145728 | tf_op jit(solution)/shard_map/all_to_all | solution.py:111
  336.0 7.1 %all-to-all-done.5 = f32[192,12,128]{2,1,0:T(8,128)} async-done(((f32[192,12,128]{2,1,0:T(8,128)}), f32[192,12,128]{2,1,0:T(8,128)}, u32[]{:S(2)}, u32[]{:S(2)}) %all-to-all-start.5) | async-done | bytes 1179680 | tf_op jit(solution)/shard_map/all_to_all | solution.py:111
  348.5 3.4 convolution_bitcast_fusion.8
  358.5 4.0 fusion.34
  362.6 4.4 fusion.38
  367.1 4.0 fusion.30
  371.1 4.8 %add_add_fusion = f32[12,192,512]{2,1,0:T(8,128)S(1)} fusion(f32[12,192,512]{2,1,0:T(8,128)S(1)} %fusion.38, f32[12,192,512]{2,1,0:T(8,128)S(1)} %fusion.30, f32[12,192,512]{2,1,0:T(8,128)S(1)} %fusion.34, f32[12,192,64]{2,1,0:T(8,128)S(1)} %get-tuple-element.9, f32[12,192,64]{2,1,0:T(8,128)S(1)} %get-tuple-element.8, f32[64,512]{1,0:T(8,128)S(1)} %copy-done.26, ...), kind=kOutput, calls=%fused_computation.4 | convolution fusion | flops 1815838720 | bytes 20316160 | tf_op jit(solution)/shard_map/xyc,cz->xyz/dot_general | solution.py:116
  378.3 3.5 multiply_reduce_fusion
  389.0 60.5 %all_to_all.159 = f32[16,144,256]{2,1,0:T(8,128)S(1)} all-to-all(f32[16,144,256]{2,1,0:T(8,128)S(1)} %copy.46), channel_id=1, replica_groups=mesh['band'=16,'pw'=16] {'band'}, dimensions={0} | all-to-all | bytes 4718592 | tf_op jit(solution)/shard_map/all_to_all | solution.py:68
  (169 shorter events, 162.3 us)
Async XLA Ops:
  3.0 40.1 %all-to-all-start = ((bf16[16,144,256]{2,1,0:T(8,128)(2,1)}), bf16[16,144,256]{2,1,0:T(8,128)(2,1)S(1)}, u32[]{:S(2)}, u32[]{:S(2)}) async-start(bf16[16,144,256]{2,1,0:T(8,128)(2,1)} %bitcast.2), calls=%async_computation | async-start | bytes 2359296 | tf_op jit(solution)/shard_map/all_to_all | solution.py:56
  44.2 5.0 %copy-start.1 = (bf16[2,12,192,256]{3,2,1,0:T(8,128)(2,1)S(1)}, bf16[2,12,192,256]{3,2,1,0:T(8,128)(2,1)}, u32[]{:S(2)}) copy-start(bf16[2,12,192,256]{3,2,1,0:T(8,128)(2,1)} %param.2) | copy-start | bytes 7077892
  44.2 34.5 %all-to-all-start.1 = ((bf16[16,144,256]{2,1,0:T(8,128)(2,1)}), bf16[16,144,256]{2,1,0:T(8,128)(2,1)S(1)}, u32[]{:S(2)}, u32[]{:S(2)}) async-start(bf16[16,144,256]{2,1,0:T(8,128)(2,1)} %broadcast_in_dim.16), calls=%async_computation.1 | async-start | bytes 2359296 | tf_op jit(solution)/shard_map/all_to_all | solution.py:59
  78.7 3.3 copy-start.13
  78.7 3.3 copy-start.23
  78.7 3.3 copy-start.24
  82.0 19.0 %copy-start = (f32[12,192,256]{2,1,0:T(8,128)}, f32[12,192,256]{2,1,0:T(8,128)S(1)}, u32[]{:S(2)}) copy-start(f32[12,192,256]{2,1,0:T(8,128)S(1)} %get-tuple-element.3) | copy-start | bytes 7077892
  88.2 2.1 copy-start.21
  88.2 2.1 copy-start.22
  98.0 3.1 copy-start.19
  98.0 3.1 copy-start.20
  113.4 29.8 %all-to-all-start.2 = ((f32[12,192,128]{2,0,1:T(8,128)}), f32[12,192,128]{2,0,1:T(8,128)}, u32[]{:S(2)}, u32[]{:S(2)}) async-start(f32[12,192,128]{2,0,1:T(8,128)} %copy.21), calls=%async_computation.2 | async-start | bytes 3145728 | tf_op jit(solution)/shard_map/all_to_all | solution.py:106
  119.6 6.0 %copy-start.4 = (f32[12,192,128]{2,1,0:T(8,128)S(1)}, f32[12,192,128]{2,1,0:T(8,128)}, u32[]{:S(2)}) copy-start(f32[12,192,128]{2,1,0:T(8,128)} %convolution_bitcast_fusion.2) | copy-start | bytes 3538948
  119.6 6.0 %copy-start.5 = (f32[12,192,128]{2,1,0:T(8,128)S(1)}, f32[12,192,128]{2,1,0:T(8,128)}, u32[]{:S(2)}) copy-start(f32[12,192,128]{2,1,0:T(8,128)} %convolution_bitcast_fusion.3) | copy-start | bytes 3538948
  143.2 29.8 %all-to-all-start.8 = ((f32[12,192,128]{2,0,1:T(8,128)}), f32[12,192,128]{2,0,1:T(8,128)}, u32[]{:S(2)}, u32[]{:S(2)}) async-start(f32[12,192,128]{2,0,1:T(8,128)} %copy.39), calls=%async_computation.8 | async-start | bytes 3145728 | tf_op jit(solution)/shard_map/all_to_all | solution.py:106
  173.1 28.4 %all-to-all-start.6 = ((f32[12,192,128]{2,0,1:T(8,128)}), f32[12,192,128]{2,0,1:T(8,128)}, u32[]{:S(2)}, u32[]{:S(2)}) async-start(f32[12,192,128]{2,0,1:T(8,128)} %copy.33), calls=%async_computation.6 | async-start | bytes 3145728 | tf_op jit(solution)/shard_map/all_to_all | solution.py:106
  201.4 28.1 %all-to-all-start.4 = ((f32[12,192,128]{2,0,1:T(8,128)}), f32[12,192,128]{2,0,1:T(8,128)}, u32[]{:S(2)}, u32[]{:S(2)}) async-start(f32[12,192,128]{2,0,1:T(8,128)} %copy.27), calls=%async_computation.4 | async-start | bytes 3145728 | tf_op jit(solution)/shard_map/all_to_all | solution.py:106
  229.6 28.2 %all-to-all-start.3 = ((f32[192,12,128]{2,1,0:T(8,128)}), f32[192,12,128]{2,1,0:T(8,128)}, u32[]{:S(2)}, u32[]{:S(2)}) async-start(f32[192,12,128]{2,1,0:T(8,128)} %copy.24), calls=%async_computation.3 | async-start | bytes 3145728 | tf_op jit(solution)/shard_map/all_to_all | solution.py:111
  235.8 1.9 copy-start.10
  257.8 28.2 %all-to-all-start.9 = ((f32[192,12,128]{2,1,0:T(8,128)}), f32[192,12,128]{2,1,0:T(8,128)}, u32[]{:S(2)}, u32[]{:S(2)}) async-start(f32[192,12,128]{2,1,0:T(8,128)} %copy.42), calls=%async_computation.9 | async-start | bytes 3145728 | tf_op jit(solution)/shard_map/all_to_all | solution.py:111
  286.0 28.4 %all-to-all-start.7 = ((f32[192,12,128]{2,1,0:T(8,128)}), f32[192,12,128]{2,1,0:T(8,128)}, u32[]{:S(2)}, u32[]{:S(2)}) async-start(f32[192,12,128]{2,1,0:T(8,128)} %copy.36), calls=%async_computation.7 | async-start | bytes 3145728 | tf_op jit(solution)/shard_map/all_to_all | solution.py:111
  302.1 4.6 %copy-start.15 = (f32[12,192,128]{2,1,0:T(8,128)}, f32[12,192,128]{2,1,0:T(8,128)S(1)}, u32[]{:S(2)}) copy-start(f32[12,192,128]{2,1,0:T(8,128)S(1)} %all_to_all.122) | copy-start | bytes 3538948
  314.4 28.7 %all-to-all-start.5 = ((f32[192,12,128]{2,1,0:T(8,128)}), f32[192,12,128]{2,1,0:T(8,128)}, u32[]{:S(2)}, u32[]{:S(2)}) async-start(f32[192,12,128]{2,1,0:T(8,128)} %copy.30), calls=%async_computation.5 | async-start | bytes 3145728 | tf_op jit(solution)/shard_map/all_to_all | solution.py:111
  327.8 3.1 copy-start.16
  348.5 3.4 copy-start.17
  358.5 4.0 copy-start.29
  358.5 4.0 copy-start.30
  362.6 4.5 copy-start.27
  362.6 4.5 copy-start.28
  367.0 4.1 copy-start.25
  367.1 4.1 copy-start.26
  375.9 2.4 copy-start.18
  (11 other events, 14.1 us)

commit v3 on v2

--- a/solution.py
+++ b/solution.py
@@ -103,12 +103,16 @@
         )
         spectrum = jnp.einsum("xyz,zc->xyc", packed, columns, precision=highest)
         spectrum = complex_pass(spectrum, cosine_y, sine_y, "uy,xyc->xuc", 1.0)
-        spectrum = lax.all_to_all(spectrum, "pw", 1, 0, tiled=True)
+        spectrum = lax.all_to_all(spectrum, "pw", 1, 1, tiled=True)
+        spectrum = spectrum.reshape(slab_rows, pw_size, rows_y, 2 * width)
+        spectrum = spectrum.transpose(1, 0, 2, 3).reshape(nx, rows_y, 2 * width)
         spectrum = complex_pass(spectrum, cosine_x, sine_x, "ux,xyc->uyc", 1.0)
         kernel = coulomb_table(nx, ny, nz, ky_first, rows_y, low, width)
         spectrum = spectrum * jnp.concatenate([kernel, kernel], -1)
-        spectrum = complex_pass(spectrum, cosine_x, sine_x, "ux,xyc->uyc", -1.0)
-        spectrum = lax.all_to_all(spectrum, "pw", 0, 1, tiled=True)
+        spectrum = complex_pass(spectrum, cosine_x, sine_x, "ux,xyc->yuc", -1.0)
+        spectrum = lax.all_to_all(spectrum, "pw", 1, 1, tiled=True)
+        spectrum = spectrum.reshape(rows_y, pw_size, slab_rows, 2 * width)
+        spectrum = spectrum.transpose(2, 1, 0, 3).reshape(slab_rows, ny, 2 * width)
         spectrum = complex_pass(spectrum, cosine_y, sine_y, "uy,xyc->xuc", -1.0)
         rows = jnp.concatenate(
             [inverse_z[low : low + width], inverse_z[nz + low : nz + low + width]], 0

time: 455 us -> 455 us (level)
    all_to_all x16 -> x0, local copies, waits for them, and re-layouts: 28.4 us -> none  [the longest x8 19.3 us: on_device(): spectrum = lax.all_to_all(spectrum, 'pw', 0, 1, tiled=True)]
    transpose x0 -> x8, local copies, waits for them, and re-layouts: none -> 18.8 us  [the longest x4 11.4 us: on_device(): spectrum = spectrum.transpose(2, 1, 0, 3).reshape(slab_rows, ny, 2 * width)]
    reshape x0 -> x8, local copies, waits for them, and re-layouts: none -> 9.63 us  [the longest x4 7.89 us: on_device(): spectrum = spectrum.transpose(2, 1, 0, 3).reshape(slab_rows, ny, 2 * width)]
  transfers between devices with their start and end apart: 10 -> 10, of which waited for: 10 -> 10; matrix products, arithmetic and copies ran while one was open for 26% -> 28% of each run, Pallas kernels for 0% -> 0%
where the time goes in v3:
time: 455 us; the launch traced here: 451 us
  waiting for transfers between devices  119 us (26%)
  matrix products  116 us (25%)
  local copies, waits for them, and re-layouts  63.7 us (14%)
  blocking collectives  60.5 us (13%)
  starting transfers between devices  56 us (12%)
  other arithmetic  33.8 us (7%)
    all_to_all x8, waiting for transfers between devices, on_device(): spectrum = lax.all_to_all(spectrum, 'pw', 1, 1, tiled=True)  69.4 us
    all_to_all x1, blocking collectives, band_reduce_scatter(): received = lax.all_to_all(pieces, 'band', 0, 0, tiled=True)  60.5 us
    dot_general x16, matrix products, complex_pass(): with_cosine = jnp.einsum(pattern, cosine_table, spectrum, precision=highest)  42.6 us
    all_to_all x8, starting transfers between devices, on_device(): spectrum = lax.all_to_all(spectrum, 'pw', 1, 1, tiled=True)  41 us
    dot_general x16, matrix products, complex_pass(): with_sine = jnp.einsum(pattern, sine_table, spectrum, precision=highest)  37.1 us
    all_to_all x1, waiting for transfers between devices, band_broadcast(): received = lax.all_to_all(pieces, 'band', 0, 0, tiled=True)  29.5 us
    all_to_all x1, waiting for transfers between devices, band_broadcast(): gathered = lax.all_to_all(spread, 'band', 0, 0, tiled=True)  19.6 us
    dot_general x4, matrix products, on_device(): spectrum = jnp.einsum('xyz,zc->xyc', packed, columns, precision=highest)  18.7 us
  transfers between devices with their start and end apart: 10, of which 10 were waited for; matrix products, arithmetic and copies ran while one was open for 28% of the time, Pallas kernels for 0%

profile of v3, /device:TPU:8, one launch (start us, length us, event | category | flops | bytes accessed | tf_op | source)
XLA Modules:
  0.0 450.6 jit_solution(13597016134165848060)
XLA Ops:
  3.0 9.9 %all-to-all-start = ((bf16[16,144,256]{2,1,0:T(8,128)(2,1)}), bf16[16,144,256]{2,1,0:T(8,128)(2,1)S(1)}, u32[]{:S(2)}, u32[]{:S(2)}) async-start(bf16[16,144,256]{2,1,0:T(8,128)(2,1)} %bitcast.2), calls=%async_computation | async-start | bytes 2359296 | tf_op jit(solution)/shard_map/all_to_all | solution.py:56
  13.6 29.5 %all-to-all-done = bf16[16,144,256]{2,1,0:T(8,128)(2,1)S(1)} async-done(((bf16[16,144,256]{2,1,0:T(8,128)(2,1)}), bf16[16,144,256]{2,1,0:T(8,128)(2,1)S(1)}, u32[]{:S(2)}, u32[]{:S(2)}) %all-to-all-start) | async-done | bytes 1179680 | tf_op jit(solution)/shard_map/all_to_all | solution.py:56
  44.2 5.0 %all-to-all-start.1 = ((bf16[16,144,256]{2,1,0:T(8,128)(2,1)}), bf16[16,144,256]{2,1,0:T(8,128)(2,1)S(1)}, u32[]{:S(2)}, u32[]{:S(2)}) async-start(bf16[16,144,256]{2,1,0:T(8,128)(2,1)} %broadcast_in_dim.16), calls=%async_computation.1 | async-start | bytes 2359296 | tf_op jit(solution)/shard_map/all_to_all | solution.py:59
  59.1 19.6 %all-to-all-done.1 = bf16[16,144,256]{2,1,0:T(8,128)(2,1)S(1)} async-done(((bf16[16,144,256]{2,1,0:T(8,128)(2,1)}), bf16[16,144,256]{2,1,0:T(8,128)(2,1)S(1)}, u32[]{:S(2)}, u32[]{:S(2)}) %all-to-all-start.1) | async-done | bytes 1179680 | tf_op jit(solution)/shard_map/all_to_all | solution.py:59
  82.1 4.1 fusion.5
  90.3 4.7 %fusion.2 = f32[12,192,128]{2,1,0:T(8,128)S(1)} fusion(f32[12,192,256]{2,1,0:T(8,128)S(1)} %get-tuple-element.3, f32[12,192,256]{2,1,0:T(8,128)S(1)} %get-tuple-element.2, f32[512,64]{1,0:T(8,128)S(1)} %copy-done.22, f32[512,64]{1,0:T(8,128)S(1)} %copy-done.21), kind=kOutput, calls=%fused_computation.11 | convolution fusion | flops 1813184512 | bytes 6160384 | tf_op jit(solution)/shard_map/xyz,zc->xyc/dot_general | solution.py:104
  101.1 4.1 fusion.3
  113.4 6.2 %all-to-all-start.2 = ((f32[12,192,128]{2,0,1:T(8,128)}), f32[12,192,128]{2,0,1:T(8,128)}, u32[]{:S(2)}, u32[]{:S(2)}) async-start(f32[12,192,128]{2,0,1:T(8,128)} %copy.21), calls=%async_computation.2 | async-start | bytes 3145728 | tf_op jit(solution)/shard_map/all_to_all | solution.py:106
  119.6 6.0 %fusion.4 = f32[12,192,128]{2,1,0:T(8,128)S(1)} fusion(f32[12,192,256]{2,1,0:T(8,128)} %copy-done, f32[12,192,256]{2,1,0:T(8,128)S(1)} %get-tuple-element.2, f32[512,64]{1,0:T(8,128)} %get-tuple-element.52, f32[512,64]{1,0:T(8,128)} %get-tuple-element.53), kind=kOutput, calls=%fused_computation.13 | convolution fusion | flops 1813184512 | bytes 6160384 | tf_op jit(solution)/shard_map/xyz,zc->xyc/dot_general | solution.py:104
  143.2 6.2 %all-to-all-start.8 = ((f32[12,192,128]{2,0,1:T(8,128)}), f32[12,192,128]{2,0,1:T(8,128)}, u32[]{:S(2)}, u32[]{:S(2)}) async-start(f32[12,192,128]{2,0,1:T(8,128)} %copy.39), calls=%async_computation.8 | async-start | bytes 3145728 | tf_op jit(solution)/shard_map/all_to_all | solution.py:106
  158.7 14.4 %all-to-all-done.8 = f32[12,192,128]{2,0,1:T(8,128)} async-done(((f32[12,192,128]{2,0,1:T(8,128)}), f32[12,192,128]{2,0,1:T(8,128)}, u32[]{:S(2)}, u32[]{:S(2)}) %all-to-all-start.8) | async-done | bytes 1179680 | tf_op jit(solution)/shard_map/all_to_all | solution.py:106
  173.1 4.8 %all-to-all-start.6 = ((f32[12,192,128]{2,0,1:T(8,128)}), f32[12,192,128]{2,0,1:T(8,128)}, u32[]{:S(2)}, u32[]{:S(2)}) async-start(f32[12,192,128]{2,0,1:T(8,128)} %copy.33), calls=%async_computation.6 | async-start | bytes 3145728 | tf_op jit(solution)/shard_map/all_to_all | solution.py:106
  177.9 4.1 convolution_bitcast_fusion.21
  190.4 11.0 %all-to-all-done.6 = f32[12,192,128]{2,0,1:T(8,128)} async-done(((f32[12,192,128]{2,0,1:T(8,128)}), f32[12,192,128]{2,0,1:T(8,128)}, u32[]{:S(2)}, u32[]{:S(2)}) %all-to-all-start.6) | async-done | bytes 1179680 | tf_op jit(solution)/shard_map/all_to_all | solution.py:106
  201.4 4.6 %all-to-all-start.4 = ((f32[12,192,128]{2,0,1:T(8,128)}), f32[12,192,128]{2,0,1:T(8,128)}, u32[]{:S(2)}, u32[]{:S(2)}) async-start(f32[12,192,128]{2,0,1:T(8,128)} %copy.27), calls=%async_computation.4 | async-start | bytes 3145728 | tf_op jit(solution)/shard_map/all_to_all | solution.py:106
  222.6 7.0 %all-to-all-done.4 = f32[12,192,128]{2,0,1:T(8,128)} async-done(((f32[12,192,128]{2,0,1:T(8,128)}), f32[12,192,128]{2,0,1:T(8,128)}, u32[]{:S(2)}, u32[]{:S(2)}) %all-to-all-start.4) | async-done | bytes 1179680 | tf_op jit(solution)/shard_map/all_to_all | solution.py:106
  229.6 4.6 %all-to-all-start.3 = ((f32[12,192,128]{2,0,1:T(8,128)}), f32[12,192,128]{2,0,1:T(8,128)}, u32[]{:S(2)}, u32[]{:S(2)}) async-start(f32[12,192,128]{2,0,1:T(8,128)} %copy.24), calls=%async_computation.3 | async-start | bytes 3145728 | tf_op jit(solution)/shard_map/all_to_all | solution.py:113
  247.2 10.6 %all-to-all-done.3 = f32[12,192,128]{2,0,1:T(8,128)} async-done(((f32[12,192,128]{2,0,1:T(8,128)}), f32[12,192,128]{2,0,1:T(8,128)}, u32[]{:S(2)}, u32[]{:S(2)}) %all-to-all-start.3) | async-done | bytes 1179680 | tf_op jit(solution)/shard_map/all_to_all | solution.py:113
  257.8 4.7 %all-to-all-start.9 = ((f32[12,192,128]{2,0,1:T(8,128)}), f32[12,192,128]{2,0,1:T(8,128)}, u32[]{:S(2)}, u32[]{:S(2)}) async-start(f32[12,192,128]{2,0,1:T(8,128)} %copy.42), calls=%async_computation.9 | async-start | bytes 3145728 | tf_op jit(solution)/shard_map/all_to_all | solution.py:113
  270.0 16.0 %all-to-all-done.9 = f32[12,192,128]{2,0,1:T(8,128)} async-done(((f32[12,192,128]{2,0,1:T(8,128)}), f32[12,192,128]{2,0,1:T(8,128)}, u32[]{:S(2)}, u32[]{:S(2)}) %all-to-all-start.9) | async-done | bytes 1179680 | tf_op jit(solution)/shard_map/all_to_all | solution.py:113
  286.0 4.9 %all-to-all-start.7 = ((f32[12,192,128]{2,0,1:T(8,128)}), f32[12,192,128]{2,0,1:T(8,128)}, u32[]{:S(2)}, u32[]{:S(2)}) async-start(f32[12,192,128]{2,0,1:T(8,128)} %copy.36), calls=%async_computation.7 | async-start | bytes 3145728 | tf_op jit(solution)/shard_map/all_to_all | solution.py:113
  290.9 4.1 convolution_bitcast_fusion.15
  308.8 3.3 convolution_bitcast_fusion.19
  314.4 5.1 %all-to-all-start.5 = ((f32[12,192,128]{2,0,1:T(8,128)}), f32[12,192,128]{2,0,1:T(8,128)}, u32[]{:S(2)}, u32[]{:S(2)}) async-start(f32[12,192,128]{2,0,1:T(8,128)} %copy.30), calls=%async_computation.5 | async-start | bytes 3145728 | tf_op jit(solution)/shard_map/all_to_all | solution.py:113
  336.0 7.1 %all-to-all-done.5 = f32[12,192,128]{2,0,1:T(8,128)} async-done(((f32[12,192,128]{2,0,1:T(8,128)}), f32[12,192,128]{2,0,1:T(8,128)}, u32[]{:S(2)}, u32[]{:S(2)}) %all-to-all-start.5) | async-done | bytes 1179680 | tf_op jit(solution)/shard_map/all_to_all | solution.py:113
  348.5 3.4 convolution_bitcast_fusion.12
  358.5 4.0 fusion.34
  362.6 4.4 fusion.38
  367.1 4.0 fusion.30
  371.1 4.8 %add_add_fusion = f32[12,192,512]{2,1,0:T(8,128)S(1)} fusion(f32[12,192,512]{2,1,0:T(8,128)S(1)} %fusion.38, f32[12,192,512]{2,1,0:T(8,128)S(1)} %fusion.30, f32[12,192,512]{2,1,0:T(8,128)S(1)} %fusion.34, f32[12,192,64]{2,1,0:T(8,128)S(1)} %get-tuple-element.9, f32[12,192,64]{2,1,0:T(8,128)S(1)} %get-tuple-element.8, f32[64,512]{1,0:T(8,128)S(1)} %copy-done.26, ...), kind=kOutput, calls=%fused_computation.4 | convolution fusion | flops 1815838720 | bytes 20316160 | tf_op jit(solution)/shard_map/xyc,cz->xyz/dot_general | solution.py:120
  378.3 3.5 multiply_reduce_fusion
  389.0 60.5 %all_to_all.55 = f32[16,144,256]{2,1,0:T(8,128)S(1)} all-to-all(f32[16,144,256]{2,1,0:T(8,128)S(1)} %copy.46), channel_id=1, replica_groups=mesh['band'=16,'pw'=16] {'band'}, dimensions={0} | all-to-all | bytes 4718592 | tf_op jit(solution)/shard_map/all_to_all | solution.py:68
  (169 shorter events, 162.3 us)
Async XLA Ops:
  3.0 40.1 %all-to-all-start = ((bf16[16,144,256]{2,1,0:T(8,128)(2,1)}), bf16[16,144,256]{2,1,0:T(8,128)(2,1)S(1)}, u32[]{:S(2)}, u32[]{:S(2)}) async-start(bf16[16,144,256]{2,1,0:T(8,128)(2,1)} %bitcast.2), calls=%async_computation | async-start | bytes 2359296 | tf_op jit(solution)/shard_map/all_to_all | solution.py:56
  44.2 5.0 %copy-start.1 = (bf16[2,12,192,256]{3,2,1,0:T(8,128)(2,1)S(1)}, bf16[2,12,192,256]{3,2,1,0:T(8,128)(2,1)}, u32[]{:S(2)}) copy-start(bf16[2,12,192,256]{3,2,1,0:T(8,128)(2,1)} %param.2) | copy-start | bytes 7077892
  44.2 34.5 %all-to-all-start.1 = ((bf16[16,144,256]{2,1,0:T(8,128)(2,1)}), bf16[16,144,256]{2,1,0:T(8,128)(2,1)S(1)}, u32[]{:S(2)}, u32[]{:S(2)}) async-start(bf16[16,144,256]{2,1,0:T(8,128)(2,1)} %broadcast_in_dim.16), calls=%async_computation.1 | async-start | bytes 2359296 | tf_op jit(solution)/shard_map/all_to_all | solution.py:59
  78.7 3.3 copy-start.13
  78.7 3.3 copy-start.23
  78.7 3.3 copy-start.24
  82.0 19.0 %copy-start = (f32[12,192,256]{2,1,0:T(8,128)}, f32[12,192,256]{2,1,0:T(8,128)S(1)}, u32[]{:S(2)}) copy-start(f32[12,192,256]{2,1,0:T(8,128)S(1)} %get-tuple-element.3) | copy-start | bytes 7077892
  88.2 2.1 copy-start.21
  88.2 2.1 copy-start.22
  98.0 3.1 copy-start.19
  98.0 3.1 copy-start.20
  113.4 29.8 %all-to-all-start.2 = ((f32[12,192,128]{2,0,1:T(8,128)}), f32[12,192,128]{2,0,1:T(8,128)}, u32[]{:S(2)}, u32[]{:S(2)}) async-start(f32[12,192,128]{2,0,1:T(8,128)} %copy.21), calls=%async_computation.2 | async-start | bytes 3145728 | tf_op jit(solution)/shard_map/all_to_all | solution.py:106
  119.6 6.0 %copy-start.4 = (f32[12,192,128]{2,1,0:T(8,128)S(1)}, f32[12,192,128]{2,1,0:T(8,128)}, u32[]{:S(2)}) copy-start(f32[12,192,128]{2,1,0:T(8,128)} %convolution_bitcast_fusion.4) | copy-start | bytes 3538948
  119.6 6.0 %copy-start.5 = (f32[12,192,128]{2,1,0:T(8,128)S(1)}, f32[12,192,128]{2,1,0:T(8,128)}, u32[]{:S(2)}) copy-start(f32[12,192,128]{2,1,0:T(8,128)} %convolution_bitcast_fusion.5) | copy-start | bytes 3538948
  143.2 29.8 %all-to-all-start.8 = ((f32[12,192,128]{2,0,1:T(8,128)}), f32[12,192,128]{2,0,1:T(8,128)}, u32[]{:S(2)}, u32[]{:S(2)}) async-start(f32[12,192,128]{2,0,1:T(8,128)} %copy.39), calls=%async_computation.8 | async-start | bytes 3145728 | tf_op jit(solution)/shard_map/all_to_all | solution.py:106
  173.1 28.4 %all-to-all-start.6 = ((f32[12,192,128]{2,0,1:T(8,128)}), f32[12,192,128]{2,0,1:T(8,128)}, u32[]{:S(2)}, u32[]{:S(2)}) async-start(f32[12,192,128]{2,0,1:T(8,128)} %copy.33), calls=%async_computation.6 | async-start | bytes 3145728 | tf_op jit(solution)/shard_map/all_to_all | solution.py:106
  201.4 28.1 %all-to-all-start.4 = ((f32[12,192,128]{2,0,1:T(8,128)}), f32[12,192,128]{2,0,1:T(8,128)}, u32[]{:S(2)}, u32[]{:S(2)}) async-start(f32[12,192,128]{2,0,1:T(8,128)} %copy.27), calls=%async_computation.4 | async-start | bytes 3145728 | tf_op jit(solution)/shard_map/all_to_all | solution.py:106
  229.6 28.2 %all-to-all-start.3 = ((f32[12,192,128]{2,0,1:T(8,128)}), f32[12,192,128]{2,0,1:T(8,128)}, u32[]{:S(2)}, u32[]{:S(2)}) async-start(f32[12,192,128]{2,0,1:T(8,128)} %copy.24), calls=%async_computation.3 | async-start | bytes 3145728 | tf_op jit(solution)/shard_map/all_to_all | solution.py:113
  235.8 1.9 copy-start.10
  257.8 28.2 %all-to-all-start.9 = ((f32[12,192,128]{2,0,1:T(8,128)}), f32[12,192,128]{2,0,1:T(8,128)}, u32[]{:S(2)}, u32[]{:S(2)}) async-start(f32[12,192,128]{2,0,1:T(8,128)} %copy.42), calls=%async_computation.9 | async-start | bytes 3145728 | tf_op jit(solution)/shard_map/all_to_all | solution.py:113
  286.0 28.4 %all-to-all-start.7 = ((f32[12,192,128]{2,0,1:T(8,128)}), f32[12,192,128]{2,0,1:T(8,128)}, u32[]{:S(2)}, u32[]{:S(2)}) async-start(f32[12,192,128]{2,0,1:T(8,128)} %copy.36), calls=%async_computation.7 | async-start | bytes 3145728 | tf_op jit(solution)/shard_map/all_to_all | solution.py:113
  302.1 4.6 %copy-start.15 = (f32[12,192,128]{2,1,0:T(8,128)}, f32[12,192,128]{2,1,0:T(8,128)S(1)}, u32[]{:S(2)}) copy-start(f32[12,192,128]{2,1,0:T(8,128)S(1)} %reshape.169) | copy-start | bytes 3538948
  314.4 28.7 %all-to-all-start.5 = ((f32[12,192,128]{2,0,1:T(8,128)}), f32[12,192,128]{2,0,1:T(8,128)}, u32[]{:S(2)}, u32[]{:S(2)}) async-start(f32[12,192,128]{2,0,1:T(8,128)} %copy.30), calls=%async_computation.5 | async-start | bytes 3145728 | tf_op jit(solution)/shard_map/all_to_all | solution.py:113
  327.8 3.1 copy-start.16
  348.5 3.4 copy-start.17
  358.5 4.0 copy-start.29
  358.5 4.0 copy-start.30
  362.6 4.5 copy-start.27
  362.6 4.5 copy-start.28
  367.1 4.1 copy-start.25
  367.1 4.1 copy-start.26
  375.9 2.4 copy-start.18
  (11 other events, 14.1 us)
